TPU v7x, 256 devices: a whole 4x4x8 slice. The times are simulated.
256 devices in a mesh: wide: 32 (over x, y, core), narrow: 8 (over z).
Axes of the slice: x: 4, y: 4, z: 8, core: 2. Of those that a mesh axis runs over, the one named last changes fastest.
Arguments:
- sources: float32 [32, 8, 16, 2, 512], P('wide', 'narrow'), may hold values from -6 to 6
- schur_blocks: bfloat16 [32, 8, 2048, 2048], P('wide', 'narrow'), as said below
- scaling: float32 [32, 8, 2, 512], P('wide', 'narrow'), may hold values from 0.08 to 0.4
- coarse_basis: float32 [32, 8, 2, 2, 8, 512], P('wide', 'narrow'), may hold values from -0.09375 to 0.09375
- coarse_inverse: float32 [32, 80, 80], P('wide'), as said below
- face_sizes: int32 [32, 8, 2], P('wide', 'narrow'), may hold values from 0 to 512, as said below
- face_match: int32 [32, 8, 2, 512], P('wide', 'narrow'), may hold values from 0 to 511, as said below
- face_slots: int32 [32, 8, 4], P('wide', 'narrow'), may hold values from 0 to 3, each once within a row
- corner_slots: int32 [33, 9], replicated, may hold values from 0 to 319, as said below
Outputs:
- solution: float32 [32, 8, 16, 2, 512], P('wide', 'narrow')
- residual: float32 [32, 8, 16, 2, 512], P('wide', 'narrow')
Inputs may be any that keep to these rules, and one draw needn't show every extreme that they name: `face_sizes`: the east faces of the last wide index and the north faces of the last narrow index have 0 unknowns; every other face has 128 to 512, and some face has exactly 512. `face_match`: each block is a permutation of 0 to 511 that maps the positions below the size of the matching owned face onto themselves. `corner_slots`: distinct slots for distinct vertices; slot 319 is used. `schur_blocks`: each block is symmetric and positive definite. `coarse_inverse`: each block is symmetric and positive definite.
All inputs are finite; a program needn't handle non-finite values.
Results may differ from a plain program's by a relative error of at most 0.0052.
Values may be sent and summed in bfloat16 or wider, within the bound.
A program may use at most 64 MiB of HBM per device.

v0:
```python
import jax
import jax.numpy as jnp
from jax import lax
from jax.sharding import PartitionSpec as P

ITERS = 2
highest = lax.Precision.HIGHEST


def shifted(block, axis, distance):
    devices = range(lax.axis_size(axis))
    route = [(i - distance, i) for i in devices if i - distance in devices]
    return lax.ppermute(block, axis, route)


def body(
    sources,
    schur_blocks,
    scaling,
    coarse_basis,
    coarse_inverse,
    face_sizes,
    face_match,
    face_slots,
    corner_slots,
):
    wide_count = lax.axis_size("wide")
    wide_at = lax.axis_index("wide")
    narrow_at = lax.axis_index("narrow")
    nrhs_count = sources.shape[2]
    face_width = sources.shape[4]
    basis_count = coarse_basis.shape[4]
    block_order = coarse_inverse.shape[1]
    capacity = block_order // basis_count
    slot_count = capacity * wide_count
    places = lax.broadcasted_iota(jnp.int32, (2, face_width), 1)
    live_mask = (places < face_sizes[0, 0][:, None]).astype(jnp.float32)
    weights = scaling[0, 0] * live_mask
    vectors = coarse_basis[0, 0] * live_mask[:, None, None, :]
    forward = face_match[0, 0]
    source_rows = lax.broadcasted_iota(jnp.int32, (2, face_width, face_width), 1)
    match_table = (forward[:, None, :] == source_rows).astype(jnp.float32)
    match_narrow = match_table.astype(jnp.bfloat16)
    slot_table = (face_slots[0, 0][:, None] == jnp.arange(4, dtype=jnp.int32)[None, :]).astype(
        jnp.float32
    )
    matrix = schur_blocks[0, 0]
    square = lax.dynamic_slice(corner_slots, (wide_at, narrow_at), (2, 2))
    corner_ids = jnp.stack([square[1, 0], square[1, 1], square[0, 1], square[1, 1]])
    incidence = (corner_ids[:, None] == jnp.arange(slot_count, dtype=jnp.int32)[None, :]).astype(
        jnp.float32
    )
    inverse_block = coarse_inverse[0]
    initial = sources[0, 0] * live_mask[None]

    def finish(residual, solved_slots):
        local_values = jnp.dot(
            incidence, solved_slots, precision=highest, preferred_element_type=jnp.float32
        )
        local_values = local_values.reshape(2, 2, basis_count, nrhs_count)
        return weights[None] * residual + jnp.einsum(
            "femk,femr->rfk", vectors, local_values, precision=highest
        )

    def precondition(residual):
        partial_value = jnp.einsum("femk,rfk->femr", vectors, residual, precision=highest).reshape(
            4, basis_count * nrhs_count
        )
        dense_part = jnp.dot(
            incidence.T, partial_value, precision=highest, preferred_element_type=jnp.float32
        )
        owned_rows = lax.psum_scatter(dense_part, "wide", scatter_dimension=0, tiled=True)
        owner_block = lax.psum(owned_rows, "narrow").reshape(block_order, nrhs_count)
        solved = jnp.dot(
            inverse_block, owner_block, precision=highest, preferred_element_type=jnp.float32
        )
        all_solved = lax.all_gather(
            solved.reshape(capacity, basis_count * nrhs_count), "wide", axis=0, tiled=True
        )
        precond = finish(residual, all_solved)
        inner_value = lax.psum(jnp.sum(residual * precond, axis=(1, 2)), ("wide", "narrow"))
        return (precond, inner_value)

    residual = initial
    solution = jnp.zeros_like(initial)
    precond, inner_now = precondition(residual)
    direction = precond
    for iteration in range(ITERS):
        rounded = direction.astype(jnp.bfloat16)
        from_west = shifted(rounded[:, 0], "wide", 1)
        from_south = shifted(rounded[:, 1], "narrow", 1)
        west_face = jnp.dot(from_west, match_narrow[0], preferred_element_type=jnp.float32)
        south_face = jnp.dot(from_south, match_narrow[1], preferred_element_type=jnp.float32)
        stacked = jnp.stack(
            [
                rounded[:, 0].astype(jnp.float32),
                rounded[:, 1].astype(jnp.float32),
                west_face,
                south_face,
            ],
            axis=1,
        )
        slotted = jnp.einsum("rdk,ds->rsk", stacked, slot_table, precision=highest).astype(
            jnp.bfloat16
        )
        product = jnp.dot(
            slotted.reshape(nrhs_count, 4 * face_width), matrix, preferred_element_type=jnp.float32
        )
        by_face = jnp.einsum(
            "rsk,ds->rdk", product.reshape(nrhs_count, 4, face_width), slot_table, precision=highest
        )
        to_west = jnp.einsum("rk,mk->rm", by_face[:, 2], match_table[0], precision=highest)
        to_south = jnp.einsum("rk,mk->rm", by_face[:, 3], match_table[1], precision=highest)
        from_east = shifted(to_west, "wide", -1)
        from_north = shifted(to_south, "narrow", -1)
        summed_all = jnp.stack([by_face[:, 0] + from_east, by_face[:, 1] + from_north], axis=1)
        applied = summed_all * live_mask[None]
        curvature = lax.psum(jnp.sum(direction * applied, axis=(1, 2)), ("wide", "narrow"))
        step_size = inner_now / curvature
        solution = solution + step_size[:, None, None] * direction
        residual = residual - step_size[:, None, None] * applied
        if iteration + 1 < ITERS:
            precond, inner_new = precondition(residual)
            direction = precond + (inner_new / inner_now)[:, None, None] * direction
            inner_now = inner_new
    return (solution[None, None], residual[None, None])


def solution(mesh):
    placed = (
        P("wide", "narrow", None, None, None),
        P("wide", "narrow", None, None),
        P("wide", "narrow", None, None),
        P("wide", "narrow", None, None, None, None),
        P("wide", None, None),
        P("wide", "narrow", None),
        P("wide", "narrow", None, None),
        P("wide", "narrow", None),
        P(),
    )
    return jax.shard_map(
        body,
        mesh=mesh,
        in_specs=placed,
        out_specs=(P("wide", "narrow", None, None, None), P("wide", "narrow", None, None, None)),
        check_vma=False,
    )
```

profile of v0, /device:TPU:1, one launch (start us, length us, event | category | flops | bytes accessed | tf_op | source)
XLA Modules:
  0.0 640.1 jit_solution(5082868968421109135)
XLA Ops:
  10.6 2.1 pad_add_fusion
  16.4 110.0 %all-reduce.6.cloned.1.call-done = f32[320,128]{1,0:T(8,128)} async-done(((f32[320,128]{1,0:T(8,128)}), f32[320,128]{1,0:T(8,128)}) %all-reduce.6.cloned.1.call-update) | async-done | bytes 163856
  127.2 23.5 %psum.42 = f32[80,16]{1,0:T(8,128)S(1)} all-reduce(f32[80,16]{1,0:T(8,128)S(1)} %reshape.170), channel_id=1, replica_groups=mesh['wide'=32,'narrow'=8] {'narrow'}, use_global_device_ids=true, to_apply=%region_1.0 | all-reduce | flops 1280 | bytes 10240 | tf_op jit(solution)/shard_map/psum | solution.py:73
  151.1 30.1 %all-gather = f32[32,10,128]{2,1,0:T(8,128)S(1)} all-gather(f32[1,10,128]{2,1,0:T(8,128)S(1)} %reshape.179), channel_id=1, replica_groups=mesh['wide'=32,'narrow'=8] {'wide'}, dimensions={0}, use_global_device_ids=true | all-gather | bytes 168960 | tf_op jit(solution)/shard_map/all_gather | solution.py:77
  182.7 1.3 collective-permute-start.1
  185.3 12.3 %copy.57 = bf16[2048,2048]{1,0:T(8,128)(2,1)} copy(bf16[2048,2048]{0,1:T(8,128)(2,1)} %bitcast.206) | data formatting | bytes 16777216 | tf_op jit(solution)/shard_map/dot_general | solution.py:106
  197.6 2.6 collective-permute-start
  201.7 5.6 fusion.60
  208.9 1.3 collective-permute-start.3
  210.2 1.9 collective-permute-start.2
  212.1 2.1 collective-permute-done.3
  214.2 1.7 collective-permute-done.2
  216.1 78.5 %all-reduce.2 = (f32[16]{0:T(128)S(1)}, f32[16]{0:T(128)S(1)}) all-reduce(f32[16]{0:T(128)S(1)} %get-tuple-element.9, f32[16]{0:T(128)S(1)} %get-tuple-element.8), channel_id=1, replica_groups=mesh['wide'=32,'narrow'=8] {'wide','narrow'}, use_global_device_ids=true, to_apply=%region_3.0 | all-reduce | flops 32 | bytes 256 | tf_op jit(solution)/shard_map/psum | solution.py:81
  296.1 106.8 %all-reduce.8.cloned.1.call-done = f32[320,128]{1,0:T(8,128)} async-done(((f32[320,128]{1,0:T(8,128)}), f32[320,128]{1,0:T(8,128)}) %all-reduce.8.cloned.1.call-update) | async-done | bytes 163856
  403.7 23.5 %psum.45 = f32[80,16]{1,0:T(8,128)S(1)} all-reduce(f32[80,16]{1,0:T(8,128)S(1)} %reshape.175), channel_id=1, replica_groups=mesh['wide'=32,'narrow'=8] {'narrow'}, use_global_device_ids=true, to_apply=%region_7.0 | all-reduce | flops 1280 | bytes 10240 | tf_op jit(solution)/shard_map/psum | solution.py:73
  427.6 30.1 %all-gather.1 = f32[32,10,128]{2,1,0:T(8,128)S(1)} all-gather(f32[1,10,128]{2,1,0:T(8,128)S(1)} %reshape.181), channel_id=1, replica_groups=mesh['wide'=32,'narrow'=8] {'wide'}, dimensions={0}, use_global_device_ids=true | all-gather | bytes 168960 | tf_op jit(solution)/shard_map/all_gather | solution.py:77
  458.5 73.3 %psum.46 = f32[16]{0:T(128)S(1)} all-reduce(f32[16]{0:T(128)S(1)} %get-tuple-element.39), channel_id=1, replica_groups=mesh['wide'=32,'narrow'=8] {'wide','narrow'}, use_global_device_ids=true, to_apply=%region_9.0 | all-reduce | flops 16 | bytes 128 | tf_op jit(solution)/shard_map/psum | solution.py:81
  531.9 2.4 collective-permute-start.4
  534.4 3.9 collective-permute-start.5
  539.5 5.6 fusion.61
  546.7 1.3 collective-permute-start.7
  548.0 2.7 collective-permute-start.6
  551.6 1.6 collective-permute-done.6
  553.5 78.3 %psum.47 = f32[16]{0:T(128)S(1)} all-reduce(f32[16]{0:T(128)S(1)} %fusion.15), channel_id=1, replica_groups=mesh['wide'=32,'narrow'=8] {'wide','narrow'}, use_global_device_ids=true, to_apply=%region_11.0 | all-reduce | flops 16 | bytes 128 | tf_op jit(solution)/shard_map/psum | solution.py:118
  (79 shorter events, 22.3 us)
Async XLA Ops:
  7.2 143.6 %copy-start = (f32[1,80,80]{2,1,0:T(8,128)S(1)}, f32[1,80,80]{2,1,0:T(8,128)}, u32[]{:S(2)}) copy-start(f32[1,80,80]{2,1,0:T(8,128)} %param.13) | copy-start | bytes 76804
  7.2 119.2 %all-reduce.6.cloned.1.call-start = ((), (), s32[]{:S(2)}) async-start(), calls=%async_computation | async-start | bytes 327680
  13.7 389.2 %all-reduce.8.cloned.1.call-start = ((), (), s32[]{:S(2)}) async-start(), calls=%async_computation.1 | async-start | bytes 327680
  182.7 17.5 %collective-permute-start.1 = (bf16[16,512]{1,0:T(8,128)(2,1)S(1)}, bf16[16,512]{1,0:T(8,128)(2,1)S(1)}, u32[]{:S(2)}, u32[]{:S(2)}) collective-permute-start(bf16[16,512]{1,0:T(8,128)(2,1)S(1)} %get-tuple-element.30), channel_id=1, source_target_pairs={{0,1},{1,2},{2,3},{3,4},{4,5},{5,6},{6,7},{8,9},{9,10},{10,11},{11... | collective-permute-start | bytes 49160 | tf_op jit(solution)/shard_map/ppermute | solution.py:13
  185.3 16.0 %copy-start.3 = (s32[1,1,4]{2,1,0:T(1,128)S(1)}, s32[1,1,4]{2,1,0:T(1,128)}, u32[]{:S(2)}) copy-start(s32[1,1,4]{2,1,0:T(1,128)} %param.16) | copy-start | bytes 52
  197.6 18.4 %copy-start.1 = (f32[1,1,16,2,512]{4,3,2,1,0:T(2,128)S(1)}, f32[1,1,16,2,512]{4,3,2,1,0:T(2,128)}, u32[]{:S(2)}) copy-start(f32[1,1,16,2,512]{4,3,2,1,0:T(2,128)} %param.9) | copy-start | bytes 196612
  197.6 97.1 %copy-start.2 = (f32[1,1,2,2,8,512]{5,4,3,2,1,0:T(8,128)S(1)}, f32[1,1,2,2,8,512]{5,4,3,2,1,0:T(8,128)}, u32[]{:S(2)}) copy-start(f32[1,1,2,2,8,512]{5,4,3,2,1,0:T(8,128)} %param.12) | copy-start | bytes 196612
  197.6 3.4 collective-permute-start
  208.9 5.4 collective-permute-start.3
  210.2 5.8 collective-permute-start.2
  531.9 6.3 collective-permute-start.4
  534.4 4.5 collective-permute-start.5
  546.7 4.9 collective-permute-start.7
  548.0 5.2 collective-permute-start.6
Sparse Core Ops, SparseCore 0:
  13.8 112.5 all-reduce.5
  296.3 106.6 all-reduce.7
where the time goes:
time: 641 us; the launch traced here: 640 us
  blocking collectives  337 us (53%)
  waiting for transfers between devices  224 us (35%)
  matrix products  21.5 us (3%)
  local copies, waits for them, and re-layouts  18.9 us (3%)
  starting transfers between devices  17.5 us (3%)
  between operations  15 us (2%)
    unnamed x4, waiting for transfers between devices  217 us
    psum x2, blocking collectives, precondition(): lax.psum(jnp.sum(residual * precond, axis=(1, 2)), ('wide', 'narrow'))  152 us
    psum x1, blocking collectives, body(): lax.psum(jnp.sum(direction * applied, axis=(1, 2)), ('wide', 'narrow'))  78.3 us
    all_gather x2, blocking collectives, precondition(): lax.all_gather(solved.reshape(capacity, basis_count * nrhs_count), 'wide'...  60.2 us
    psum x2, blocking collectives, precondition(): lax.psum(owned_rows, 'narrow').reshape(block_order, nrhs_count)  47.1 us
    ppermute x8, starting transfers between devices, shifted(): return lax.ppermute(block, axis, route)  17.5 us
  transfers between devices with their start and end apart: 10, of which 8 were waited for; matrix products, arithmetic and copies ran while one was open for 2% of the time, Pallas kernels for 0%

commit v1 on v0

--- a/solution.py
+++ b/solution.py
@@ -78,7 +78,8 @@
             solved.reshape(capacity, basis_count * nrhs_count), "wide", axis=0, tiled=True
         )
         precond = finish(residual, all_solved)
-        inner_value = lax.psum(jnp.sum(residual * precond, axis=(1, 2)), ("wide", "narrow"))
+        inner = lax.psum(jnp.sum(residual * precond, axis=(1, 2)), "wide")
+        inner_value = lax.psum(inner, "narrow")
         return (precond, inner_value)
 
     residual = initial

time: 641 us -> 721 us (1.12)
  blocking collectives: 337 us -> 412 us
    psum x1 -> x2, blocking collectives: 78.3 us -> 155 us  [body(): lax.psum(jnp.sum(direction * applied, axis=(1, 2)), ('wide', 'narrow'))]
    psum x2 -> x4, blocking collectives: 152 us -> 150 us  [the longest x2 125 us: precondition(): inner = lax.psum(jnp.sum(residual * precond, axis=(1, 2)), 'wide')]
  transfers between devices with their start and end apart: 10 -> 10, of which waited for: 8 -> 7; matrix products, arithmetic and copies ran while one was open for 2% -> 2% of each run, Pallas kernels for 0% -> 0%
where the time goes in v1:
time: 721 us; the launch traced here: 719 us
  blocking collectives  412 us (57%)
  waiting for transfers between devices  225 us (31%)
  starting transfers between devices  21.7 us (3%)
  matrix products  21.6 us (3%)
  local copies, waits for them, and re-layouts  18.9 us (3%)
  between operations  15 us (2%)
    unnamed x4, waiting for transfers between devices  218 us
    psum x2, blocking collectives, body(): lax.psum(jnp.sum(direction * applied, axis=(1, 2)), ('wide', 'narrow'))  155 us
    psum x2, blocking collectives, precondition(): inner = lax.psum(jnp.sum(residual * precond, axis=(1, 2)), 'wide')  125 us
    all_gather x2, blocking collectives, precondition(): lax.all_gather(solved.reshape(capacity, basis_count * nrhs_count), 'wide'...  60.2 us
    psum x2, blocking collectives, precondition(): lax.psum(owned_rows, 'narrow').reshape(block_order, nrhs_count)  47.1 us
    psum x2, blocking collectives, precondition(): inner_value = lax.psum(inner, 'narrow')  24.9 us
    ppermute x8, starting transfers between devices, shifted(): return lax.ppermute(block, axis, route)  21.6 us
  transfers between devices with their start and end apart: 10, of which 7 were waited for; matrix products, arithmetic and copies ran while one was open for 2% of the time, Pallas kernels for 0%

profile of v1, /device:TPU:1, one launch (start us, length us, event | category | flops | bytes accessed | tf_op | source)
XLA Modules:
  0.0 719.4 jit_solution(11488864051746506509)
XLA Ops:
  10.6 2.1 pad_add_fusion
  16.4 110.0 %all-reduce.5.cloned.1.call-done = f32[320,128]{1,0:T(8,128)} async-done(((f32[320,128]{1,0:T(8,128)}), f32[320,128]{1,0:T(8,128)}) %all-reduce.5.cloned.1.call-update) | async-done | bytes 163856
  127.2 23.5 %psum.56 = f32[80,16]{1,0:T(8,128)S(1)} all-reduce(f32[80,16]{1,0:T(8,128)S(1)} %reshape.170), channel_id=1, replica_groups=mesh['wide'=32,'narrow'=8] {'narrow'}, use_global_device_ids=true, to_apply=%region_1.0 | all-reduce | flops 1280 | bytes 10240 | tf_op jit(solution)/shard_map/psum | solution.py:73
  151.1 30.1 %all-gather = f32[32,10,128]{2,1,0:T(8,128)S(1)} all-gather(f32[1,10,128]{2,1,0:T(8,128)S(1)} %reshape.179), channel_id=1, replica_groups=mesh['wide'=32,'narrow'=8] {'wide'}, dimensions={0}, use_global_device_ids=true | all-gather | bytes 168960 | tf_op jit(solution)/shard_map/all_gather | solution.py:77
  182.7 1.3 collective-permute-start.1
  185.3 12.3 %copy.57 = bf16[2048,2048]{1,0:T(8,128)(2,1)} copy(bf16[2048,2048]{0,1:T(8,128)(2,1)} %bitcast.206) | data formatting | bytes 16777216 | tf_op jit(solution)/shard_map/dot_general | solution.py:107
  197.6 2.6 collective-permute-start
  201.7 5.6 fusion.60
  210.2 1.9 collective-permute-start.2
  212.1 2.1 collective-permute-done.3
  214.2 1.7 collective-permute-done.2
  216.1 78.6 %psum.59 = f32[16]{0:T(128)S(1)} all-reduce(f32[16]{0:T(128)S(1)} %get-tuple-element.8), channel_id=1, replica_groups=mesh['wide'=32,'narrow'=8] {'wide','narrow'}, use_global_device_ids=true, to_apply=%region_6.0 | all-reduce | flops 16 | bytes 128 | tf_op jit(solution)/shard_map/psum | solution.py:119
  294.7 62.7 %psum.57 = f32[16]{0:T(128)S(1)} all-reduce(f32[16]{0:T(128)S(1)} %get-tuple-element.9), channel_id=1, replica_groups=mesh['wide'=32,'narrow'=8] {'wide'}, use_global_device_ids=true, to_apply=%region_3.0 | all-reduce | flops 16 | bytes 128 | tf_op jit(solution)/shard_map/psum | solution.py:81
  357.4 13.4 %psum.58 = f32[16]{0:T(128)S(1)} all-reduce(f32[16]{0:T(128)S(1)} %psum.57), channel_id=1, replica_groups=mesh['wide'=32,'narrow'=8] {'narrow'}, use_global_device_ids=true, to_apply=%region_4.0 | all-reduce | flops 16 | bytes 128 | tf_op jit(solution)/shard_map/psum | solution.py:82
  372.3 108.1 %all-reduce.7.cloned.1.call-done = f32[320,128]{1,0:T(8,128)} async-done(((f32[320,128]{1,0:T(8,128)}), f32[320,128]{1,0:T(8,128)}) %all-reduce.7.cloned.1.call-update) | async-done | bytes 163856
  481.2 23.5 %psum.60 = f32[80,16]{1,0:T(8,128)S(1)} all-reduce(f32[80,16]{1,0:T(8,128)S(1)} %reshape.175), channel_id=1, replica_groups=mesh['wide'=32,'narrow'=8] {'narrow'}, use_global_device_ids=true, to_apply=%region_8.0 | all-reduce | flops 1280 | bytes 10240 | tf_op jit(solution)/shard_map/psum | solution.py:73
  505.1 30.1 %all-gather.1 = f32[32,10,128]{2,1,0:T(8,128)S(1)} all-gather(f32[1,10,128]{2,1,0:T(8,128)S(1)} %reshape.181), channel_id=1, replica_groups=mesh['wide'=32,'narrow'=8] {'wide'}, dimensions={0}, use_global_device_ids=true | all-gather | bytes 168960 | tf_op jit(solution)/shard_map/all_gather | solution.py:77
  536.0 62.2 %psum.61 = f32[16]{0:T(128)S(1)} all-reduce(f32[16]{0:T(128)S(1)} %get-tuple-element.37), channel_id=1, replica_groups=mesh['wide'=32,'narrow'=8] {'wide'}, use_global_device_ids=true, to_apply=%region_10.0 | all-reduce | flops 16 | bytes 128 | tf_op jit(solution)/shard_map/psum | solution.py:81
  598.2 11.5 %psum.62 = f32[16]{0:T(128)S(1)} all-reduce(f32[16]{0:T(128)S(1)} %psum.61), channel_id=1, replica_groups=mesh['wide'=32,'narrow'=8] {'narrow'}, use_global_device_ids=true, to_apply=%region_11.0 | all-reduce | flops 16 | bytes 128 | tf_op jit(solution)/shard_map/psum | solution.py:82
  609.8 4.8 collective-permute-start.4
  614.5 2.9 collective-permute-start.5
  619.4 5.6 fusion.61
  627.8 5.5 collective-permute-start.6
  634.4 76.6 %psum.63 = f32[16]{0:T(128)S(1)} all-reduce(f32[16]{0:T(128)S(1)} %fusion.15), channel_id=1, replica_groups=mesh['wide'=32,'narrow'=8] {'wide','narrow'}, use_global_device_ids=true, to_apply=%region_13.0 | all-reduce | flops 16 | bytes 128 | tf_op jit(solution)/shard_map/psum | solution.py:119
  (82 shorter events, 25.5 us)
Async XLA Ops:
  7.2 143.6 %copy-start = (f32[1,80,80]{2,1,0:T(8,128)S(1)}, f32[1,80,80]{2,1,0:T(8,128)}, u32[]{:S(2)}) copy-start(f32[1,80,80]{2,1,0:T(8,128)} %param.13) | copy-start | bytes 76804
  7.2 119.2 %all-reduce.5.cloned.1.call-start = ((), (), s32[]{:S(2)}) async-start(), calls=%async_computation | async-start | bytes 327680
  13.7 466.7 %all-reduce.7.cloned.1.call-start = ((), (), s32[]{:S(2)}) async-start(), calls=%async_computation.1 | async-start | bytes 327680
  182.7 17.5 %collective-permute-start.1 = (bf16[16,512]{1,0:T(8,128)(2,1)S(1)}, bf16[16,512]{1,0:T(8,128)(2,1)S(1)}, u32[]{:S(2)}, u32[]{:S(2)}) collective-permute-start(bf16[16,512]{1,0:T(8,128)(2,1)S(1)} %get-tuple-element.28), channel_id=1, source_target_pairs={{0,1},{1,2},{2,3},{3,4},{4,5},{5,6},{6,7},{8,9},{9,10},{10,11},{11... | collective-permute-start | bytes 49160 | tf_op jit(solution)/shard_map/ppermute | solution.py:13
  185.3 16.0 %copy-start.3 = (s32[1,1,4]{2,1,0:T(1,128)S(1)}, s32[1,1,4]{2,1,0:T(1,128)}, u32[]{:S(2)}) copy-start(s32[1,1,4]{2,1,0:T(1,128)} %param.16) | copy-start | bytes 52
  197.6 18.4 %copy-start.1 = (f32[1,1,16,2,512]{4,3,2,1,0:T(2,128)S(1)}, f32[1,1,16,2,512]{4,3,2,1,0:T(2,128)}, u32[]{:S(2)}) copy-start(f32[1,1,16,2,512]{4,3,2,1,0:T(2,128)} %param.9) | copy-start | bytes 196612
  197.6 173.2 %copy-start.2 = (f32[1,1,2,2,8,512]{5,4,3,2,1,0:T(8,128)S(1)}, f32[1,1,2,2,8,512]{5,4,3,2,1,0:T(8,128)}, u32[]{:S(2)}) copy-start(f32[1,1,2,2,8,512]{5,4,3,2,1,0:T(8,128)} %param.12) | copy-start | bytes 196612
  197.6 3.4 collective-permute-start
  208.9 5.4 collective-permute-start.3
  210.2 5.8 collective-permute-start.2
  609.8 8.7 %collective-permute-start.4 = (bf16[16,512]{1,0:T(8,128)(2,1)S(1)}, bf16[16,512]{1,0:T(8,128)(2,1)S(1)}, u32[]{:S(2)}, u32[]{:S(2)}) collective-permute-start(bf16[16,512]{1,0:T(8,128)(2,1)S(1)} %get-tuple-element.23), channel_id=1, source_target_pairs={{0,8},{8,16},{16,24},{24,32},{32,40},{40,48},{48,56},{56,64},{64,7... | collective-permute-start | bytes 49160 | tf_op jit(solution)/shard_map/ppermute | solution.py:13
  614.5 4.2 collective-permute-start.5
  626.5 6.8 collective-permute-start.7
  627.8 6.4 collective-permute-start.6
Sparse Core Ops, SparseCore 0:
  13.8 112.5 all-reduce.4
  372.4 107.9 all-reduce.6
